TPU v7x, 32 devices: a whole 2x2x4 slice. The times are simulated.
32 devices in a mesh: row: 8 (over z, x), col: 4 (over y, core).
Axes of the slice: x: 2, y: 2, z: 4, core: 2. Of those that a mesh axis runs over, the one named last changes fastest.
Arguments:
- vectors: float32 [8, 4096], P(None, ('row', 'col')), may hold values from -6 to 6
- values: float32 [512, 16384], P('row', 'col'), may hold values from -1 to 1
- block_rows: int32 [8, 256], P('row', 'col'), may hold values from 0 to 7
- block_cols: int32 [8, 256], P('row', 'col'), may hold values from 0 to 15
- counts: int32 [8, 4], P('row', 'col'), may hold values from 16 to 64, as said below
Outputs:
- product: float32 [8, 4096], P(None, ('row', 'col'))
Inputs may be any that keep to these rules, and one draw needn't show every extreme that they name: counts[r, c] slots of tile (r, c) hold blocks, the others are unused; some tile uses all 64 slots.
All inputs are finite; a program needn't handle non-finite values.
Results may differ from a plain program's by a relative error of at most 0.0003.
Values sent between devices are 32-bit elements; how exact they have to be, the bound alone decides.
No kernel may reach another device: no remote copies, remote signals or barrier semaphores. Data moves between devices by JAX's collectives and lax.ppermute only.
A program may use at most 64 MiB of HBM per device.

v0:
```python
import jax
import jax.numpy as jnp
from jax import lax
from jax.sharding import PartitionSpec as P

BLK = 64


def tile_terms(blocks, rows, cols, count, row_seg, col_seg):
    highest = lax.Precision.HIGHEST
    slots = blocks.shape[0]
    nvec = row_seg.shape[0]
    row_blocks = row_seg.shape[1] // blocks.shape[1]
    col_blocks = col_seg.shape[1] // blocks.shape[1]
    width = blocks.shape[1]
    live = (jnp.arange(slots, dtype=jnp.int32) < count).astype(jnp.float32)
    row_hits = (rows[:, None] == jnp.arange(row_blocks, dtype=jnp.int32)[None, :]).astype(
        jnp.float32
    ) * live[:, None]
    col_hits = (cols[:, None] == jnp.arange(col_blocks, dtype=jnp.int32)[None, :]).astype(
        jnp.float32
    ) * live[:, None]
    row_parts = row_seg.reshape(nvec, row_blocks, width)
    col_parts = col_seg.reshape(nvec, col_blocks, width)
    col_pick = jnp.take(col_parts, cols, axis=1)
    row_pick = jnp.take(row_parts, rows, axis=1)
    plain = jnp.einsum("kij,vkj->vki", blocks, col_pick, precision=highest)
    turned = jnp.einsum("kji,vkj->vki", blocks, row_pick, precision=highest)
    plain_part = jnp.einsum("kb,vki->vbi", row_hits, plain, precision=highest).reshape(
        nvec, row_blocks * width
    )
    turned_part = jnp.einsum("kb,vki->vbi", col_hits, turned, precision=highest).reshape(
        nvec, col_blocks * width
    )
    return (plain_part, turned_part)


def sum_rows(plain_part):
    return lax.psum_scatter(plain_part, "col", scatter_dimension=1, tiled=True)


def sum_columns(turned_part):
    return lax.psum_scatter(turned_part, "row", scatter_dimension=1, tiled=True)


def per_device(vectors, values, block_rows, block_cols, counts):
    row_seg = lax.all_gather(vectors, "col", axis=1, tiled=True)
    col_seg = lax.all_gather(vectors, "row", axis=1, tiled=True)
    blocks = values.reshape(values.shape[0], BLK, BLK)
    rows = block_rows[0]
    cols = block_cols[0]
    count = counts[0, 0]
    plain_part, turned_part = tile_terms(blocks, rows, cols, count, row_seg, col_seg)
    plain_sum = sum_rows(plain_part)
    turned_sum = sum_columns(turned_part)
    return plain_sum + turned_sum


def solution(mesh):
    in_specs = (
        P(None, ("row", "col")),
        P("row", "col"),
        P("row", "col"),
        P("row", "col"),
        P("row", "col"),
    )
    out_specs = P(None, ("row", "col"))
    return jax.shard_map(
        per_device, mesh=mesh, in_specs=in_specs, out_specs=out_specs, check_vma=False
    )
```

profile of v0, /device:TPU:0, one launch (start us, length us, event | category | flops | bytes accessed | tf_op | source)
XLA Modules:
  0.0 134.8 jit_solution(16836529348863672988)
XLA Ops:
  6.5 0.0 reduce-scatter.3.cloned.1.call-start
  6.5 0.7 fusion.20
  7.2 0.7 compare_and_fusion.1
  7.9 2.0 %reshape.91 = f32[64,64,64]{2,1,0:T(8,128)S(1)} reshape(f32[64,4096]{1,0:T(8,128)} %param.6) | data formatting | bytes 2097152 | tf_op jit(solution)/shard_map/reshape | solution.py:49
  9.9 0.0 copy-done
  9.9 0.0 copy-start.1
  9.9 32.4 %all_gather.6 = f32[8,1024]{1,0:T(8,128)S(1)} all-gather(f32[8,128]{1,0:T(8,128)S(1)} %copy-done), channel_id=1, replica_groups=mesh['row'=8,'col'=4] {'row'}, dimensions={1}, use_global_device_ids=true | all-gather | bytes 36864 | tf_op jit(solution)/shard_map/all_gather | solution.py:48
  42.3 0.1 reshape.90
  43.1 0.6 gather_fusion
  43.7 3.4 %convolution_bitcast_fusion.1 = f32[8,64,64]{2,0,1:T(8,128)S(1)} fusion(f32[64,64,64]{2,1,0:T(8,128)S(1)} %reshape.91, f32[64,8,64]{2,1,0:T(8,128)S(1)} %gather_fusion, pred[64]{0:T(512)(128)(4,1)S(1)} %compare_and_fusion.1), kind=kOutput, calls=%fused_computation.3 | convolution fusion | flops 25198592 | bytes 1310784 | tf_op jit(solution)/shard_map/kij,vkj->vki/dot_general | solution.py:27
  47.2 0.3 convolution_bitcast_fusion.3
  47.4 0.7 reshape.92
  48.1 0.0 reduce-scatter.3.cloned.1.call-update
  48.1 0.0 reduce-scatter.5.cloned.1.call-start
  48.2 5.2 %all_gather.7 = f32[8,512]{1,0:T(8,128)S(1)} all-gather(f32[8,128]{1,0:T(8,128)S(1)} %copy-done), channel_id=1, replica_groups=mesh['row'=8,'col'=4] {'col'}, dimensions={1}, use_global_device_ids=true | all-gather | bytes 20480 | tf_op jit(solution)/shard_map/all_gather | solution.py:47
  53.4 0.1 reshape.93
  53.5 0.6 gather_fusion.1
  54.1 1.9 %convolution_bitcast_fusion = f32[8,64,64]{2,0,1:T(8,128)S(1)} fusion(f32[64,64,64]{2,1,0:T(8,128)S(1)} %reshape.91, f32[64,8,64]{2,1,0:T(8,128)S(1)} %gather_fusion.1, pred[64]{0:T(512)(128)(4,1)S(1)} %compare_and_fusion), kind=kOutput, calls=%fused_computation.2 | convolution fusion | flops 25198592 | bytes 1310784 | tf_op jit(solution)/shard_map/kji,vkj->vki/dot_general | solution.py:28
  56.1 0.3 convolution_bitcast_fusion.2
  56.3 0.7 reshape.94
  57.0 0.0 reduce-scatter.5.cloned.1.call-update
  57.0 11.7 %reduce-scatter.3.cloned.1.call-done = f32[8,128]{1,0:T(8,128)} async-done(((f32[8,512]{1,0:T(8,128)}), f32[8,128]{1,0:T(8,128)}) %reduce-scatter.3.cloned.1.call-update) | async-done | bytes 4112 | tf_op jit(solution)/shard_map/reduce_scatter | solution.py:39
  68.7 57.9 %reduce-scatter.5.cloned.1.call-done = f32[8,128]{1,0:T(8,128)} async-done(((f32[8,1024]{1,0:T(8,128)}), f32[8,128]{1,0:T(8,128)}) %reduce-scatter.5.cloned.1.call-update) | async-done | bytes 4112 | tf_op jit(solution)/shard_map/reduce_scatter | solution.py:43
  126.6 1.3 add.57
  (11 shorter events, 0.1 us)
Async XLA Ops:
  6.5 3.3 %copy-start = (f32[8,128]{1,0:T(8,128)S(1)}, f32[8,128]{1,0:T(8,128)}, u32[]{:S(2)}) copy-start(f32[8,128]{1,0:T(8,128)} %param.5) | copy-start | bytes 12292
  6.5 62.2 %reduce-scatter.3.cloned.1.call-start = ((), (), s32[]{:S(2)}) async-start(), calls=%async_computation.2 | async-start | bytes 20480 | tf_op jit(solution)/shard_map/reduce_scatter | solution.py:39
  9.9 37.3 %copy-start.1 = (s32[1,64]{1,0:T(1,128)S(1)}, s32[1,64]{1,0:T(1,128)}, u32[]{:S(2)}) copy-start(s32[1,64]{1,0:T(1,128)} %param.7) | copy-start | bytes 772
  47.1 8.9 %copy-start.2 = (s32[1,64]{1,0:T(1,128)S(1)}, s32[1,64]{1,0:T(1,128)}, u32[]{:S(2)}) copy-start(s32[1,64]{1,0:T(1,128)} %param.8) | copy-start | bytes 772
  48.1 78.5 %reduce-scatter.5.cloned.1.call-start = ((), (), s32[]{:S(2)}) async-start(), calls=%async_computation.3 | async-start | bytes 36864 | tf_op jit(solution)/shard_map/reduce_scatter | solution.py:43
Sparse Core Ops, SparseCore 0:
  48.3 20.4 reduce-scatter.2
  71.9 54.7 reduce-scatter.4
where the time goes:
time: 135 us
  waiting for transfers between devices  69.6 us (52%)
  blocking collectives  37.6 us (28%)
  between operations  14.1 us (10%)
  matrix products  5.88 us (4%)
  local copies, waits for them, and re-layouts  4.82 us (4%)
  other arithmetic  2.63 us (2%)
    reduce_scatter x1, waiting for transfers between devices, sum_columns(): return lax.psum_scatter(turned_part, 'row', scatter_dimension=1, tiled=True)  57.9 us
    all_gather x1, blocking collectives, per_device(): col_seg = lax.all_gather(vectors, 'row', axis=1, tiled=True)  32.4 us
    reduce_scatter x1, waiting for transfers between devices, sum_rows(): return lax.psum_scatter(plain_part, 'col', scatter_dimension=1, tiled=True)  11.7 us
    all_gather x1, blocking collectives, per_device(): row_seg = lax.all_gather(vectors, 'col', axis=1, tiled=True)  5.21 us
    dot_general x1, matrix products, tile_terms(): plain = jnp.einsum('kij,vkj->vki', blocks, col_pick, precision=highest)  3.41 us
  transfers between devices with their start and end apart: 2, of which 2 were waited for; matrix products, arithmetic and copies ran while one was open for 3% of the time, Pallas kernels for 0%

commit v1 on v0

--- a/solution.py
+++ b/solution.py
@@ -45,7 +45,9 @@
 
 def per_device(vectors, values, block_rows, block_cols, counts):
     row_seg = lax.all_gather(vectors, "col", axis=1, tiled=True)
-    col_seg = lax.all_gather(vectors, "row", axis=1, tiled=True)
+    col_seg = jnp.concatenate(
+        lax.all_to_all(jnp.stack([vectors] * lax.axis_size("row")), "row", 0, 0), axis=1
+    )
     blocks = values.reshape(values.shape[0], BLK, BLK)
     rows = block_rows[0]
     cols = block_cols[0]

time: 135 us -> 114 us (0.84)
  blocking collectives: 37.6 us -> 5.34 us
  starting transfers between devices: 0.04 us -> 7.36 us
  waiting for transfers between devices: 69.6 us -> 72.1 us
    all_gather x1 -> x0, blocking collectives: 32.4 us -> none  [per_device(): col_seg = lax.all_gather(vectors, 'row', axis=1, tiled=True)]
    reduce_scatter x1, waiting for transfers between devices: 11.7 us -> 21 us  [sum_rows(): return lax.psum_scatter(plain_part, 'col', scatter_dimension=1, tiled=True)]
    all_to_all x0 -> x1, starting transfers between devices: none -> 7.28 us  [per_device(): lax.all_to_all(jnp.stack([vectors] * lax.axis_size('row')), 'row', 0, 0)]
    reduce_scatter x1, waiting for transfers between devices: 57.9 us -> 51.1 us  [sum_columns(): return lax.psum_scatter(turned_part, 'row', scatter_dimension=1, tiled=True)]
    another operation x0 -> x3, local copies, waits for them, and re-layouts: none -> 1.4 us  [the longest x1 1.3 us: per_device(): jnp.stack([vectors] * lax.axis_size('row'))]
  transfers between devices with their start and end apart: 2 -> 3, of which waited for: 2 -> 2; matrix products, arithmetic and copies ran while one was open for 3% -> 11% of each run, Pallas kernels for 0% -> 0%
where the time goes in v1:
time: 114 us
  waiting for transfers between devices  72.1 us (63%)
  between operations  14.2 us (12%)
  starting transfers between devices  7.36 us (6%)
  local copies, waits for them, and re-layouts  6.13 us (5%)
  matrix products  5.87 us (5%)
  blocking collectives  5.34 us (5%)
  other arithmetic  2.63 us (2%)
    reduce_scatter x1, waiting for transfers between devices, sum_columns(): return lax.psum_scatter(turned_part, 'row', scatter_dimension=1, tiled=True)  51.1 us
    reduce_scatter x1, waiting for transfers between devices, sum_rows(): return lax.psum_scatter(plain_part, 'col', scatter_dimension=1, tiled=True)  21 us
    all_to_all x1, starting transfers between devices, per_device(): lax.all_to_all(jnp.stack([vectors] * lax.axis_size('row')), 'row', 0, 0)  7.28 us
    all_gather x1, blocking collectives, per_device(): row_seg = lax.all_gather(vectors, 'col', axis=1, tiled=True)  5.34 us
    dot_general x1, matrix products, tile_terms(): plain = jnp.einsum('kij,vkj->vki', blocks, col_pick, precision=highest)  3.41 us
  transfers between devices with their start and end apart: 3, of which 2 were waited for; matrix products, arithmetic and copies ran while one was open for 11% of the time, Pallas kernels for 0%

profile of v1, /device:TPU:0, one launch (start us, length us, event | category | flops | bytes accessed | tf_op | source)
XLA Modules:
  0.0 113.6 jit_solution(4250208358968856334)
XLA Ops:
  6.5 1.3 %stack.2 = f32[8,8,128]{2,1,0:T(8,128)} broadcast(f32[8,128]{1,0:T(8,128)} %param.5), dimensions={1,2} | broadcast | bytes 36864 | tf_op jit(solution)/shard_map/stack | solution.py:49
  7.8 7.3 %all-to-all-start = ((f32[8,8,128]{2,1,0:T(8,128)}), f32[8,8,128]{2,1,0:T(8,128)S(1)}, u32[]{:S(2)}, u32[]{:S(2)}) async-start(f32[8,8,128]{2,1,0:T(8,128)} %stack.2), calls=%async_computation | async-start | bytes 65536 | tf_op jit(solution)/shard_map/all_to_all | solution.py:49
  15.1 0.0 reduce-scatter.5.cloned.1.call-start
  15.2 5.3 %all_gather.3 = f32[8,512]{1,0:T(8,128)S(1)} all-gather(f32[8,128]{1,0:T(8,128)} %param.5), channel_id=1, replica_groups=mesh['row'=8,'col'=4] {'col'}, dimensions={1}, use_global_device_ids=true | all-gather | bytes 20480 | tf_op jit(solution)/shard_map/all_gather | solution.py:47
  20.5 0.7 fusion.21
  21.2 0.7 compare_and_fusion
  21.8 2.0 %reshape.93 = f32[64,64,64]{2,1,0:T(8,128)S(1)} reshape(f32[64,4096]{1,0:T(8,128)} %param.6) | data formatting | bytes 2097152 | tf_op jit(solution)/shard_map/reshape | solution.py:51
  23.8 0.0 copy-start
  24.5 0.1 reshape.95
  24.6 0.6 gather_fusion.1
  25.2 1.9 %convolution_bitcast_fusion = f32[8,64,64]{2,0,1:T(8,128)S(1)} fusion(f32[64,64,64]{2,1,0:T(8,128)S(1)} %reshape.93, f32[64,8,64]{2,1,0:T(8,128)S(1)} %gather_fusion.1, pred[64]{0:T(512)(128)(4,1)S(1)} %compare_and_fusion), kind=kOutput, calls=%fused_computation.2 | convolution fusion | flops 25198592 | bytes 1310784 | tf_op jit(solution)/shard_map/kji,vkj->vki/dot_general | solution.py:28
  27.2 0.3 convolution_bitcast_fusion.2
  27.5 0.7 reshape.96
  28.1 0.0 reduce-scatter.5.cloned.1.call-update
  28.2 0.0 reduce-scatter.3.cloned.1.call-start
  28.3 0.1 reshape_reshape.3
  28.4 0.6 gather_fusion
  29.0 3.4 %convolution_bitcast_fusion.1 = f32[8,64,64]{2,0,1:T(8,128)S(1)} fusion(f32[64,64,64]{2,1,0:T(8,128)S(1)} %reshape.93, f32[64,8,64]{2,1,0:T(8,128)S(1)} %gather_fusion, pred[64]{0:T(512)(128)(4,1)S(1)} %compare_and_fusion.1), kind=kOutput, calls=%fused_computation.3 | convolution fusion | flops 25198592 | bytes 1310784 | tf_op jit(solution)/shard_map/kij,vkj->vki/dot_general | solution.py:27
  32.4 0.3 convolution_bitcast_fusion.3
  32.7 0.7 reshape.94
  33.4 0.0 reduce-scatter.3.cloned.1.call-update
  33.4 51.1 %reduce-scatter.5.cloned.1.call-done = f32[8,128]{1,0:T(8,128)} async-done(((f32[8,1024]{1,0:T(8,128)}), f32[8,128]{1,0:T(8,128)}) %reduce-scatter.5.cloned.1.call-update) | async-done | bytes 4112 | tf_op jit(solution)/shard_map/reduce_scatter | solution.py:43
  84.5 21.0 %reduce-scatter.3.cloned.1.call-done = f32[8,128]{1,0:T(8,128)} async-done(((f32[8,512]{1,0:T(8,128)}), f32[8,128]{1,0:T(8,128)}) %reduce-scatter.3.cloned.1.call-update) | async-done | bytes 4112 | tf_op jit(solution)/shard_map/reduce_scatter | solution.py:39
  105.5 1.3 %add.57 = f32[8,128]{1,0:T(8,128)} add(f32[8,128]{1,0:T(8,128)} %reduce-scatter.3.cloned.1.call-done, f32[8,128]{1,0:T(8,128)} %reduce-scatter.5.cloned.1.call-done) | non-fusion elementwise | flops 1024 | bytes 12288 | tf_op jit(solution)/shard_map/add | solution.py:58
  (12 shorter events, 0.1 us)
Async XLA Ops:
  7.8 20.4 %all-to-all-start = ((f32[8,8,128]{2,1,0:T(8,128)}), f32[8,8,128]{2,1,0:T(8,128)S(1)}, u32[]{:S(2)}, u32[]{:S(2)}) async-start(f32[8,8,128]{2,1,0:T(8,128)} %stack.2), calls=%async_computation | async-start | bytes 65536 | tf_op jit(solution)/shard_map/all_to_all | solution.py:49
  15.1 69.4 %reduce-scatter.5.cloned.1.call-start = ((), (), s32[]{:S(2)}) async-start(), calls=%async_computation.4 | async-start | bytes 36864 | tf_op jit(solution)/shard_map/reduce_scatter | solution.py:43
  23.8 3.3 %copy-start = (s32[1,64]{1,0:T(1,128)S(1)}, s32[1,64]{1,0:T(1,128)}, u32[]{:S(2)}) copy-start(s32[1,64]{1,0:T(1,128)} %param.8) | copy-start | bytes 772
  27.2 5.3 %copy-start.1 = (s32[1,64]{1,0:T(1,128)S(1)}, s32[1,64]{1,0:T(1,128)}, u32[]{:S(2)}) copy-start(s32[1,64]{1,0:T(1,128)} %param.7) | copy-start | bytes 772
  28.2 77.3 %reduce-scatter.3.cloned.1.call-start = ((), (), s32[]{:S(2)}) async-start(), calls=%async_computation.3 | async-start | bytes 20480 | tf_op jit(solution)/shard_map/reduce_scatter | solution.py:39
Sparse Core Ops, SparseCore 0:
  28.3 56.1 reduce-scatter.4
  86.9 18.5 reduce-scatter.2
